TPU v7x, 32 devices: a whole 2x2x4 slice. The times are simulated.
32 devices in a mesh: view: 4 (over x, core), samp: 8 (over z, y).
Axes of the slice: x: 2, y: 2, z: 4, core: 2. Of those that a mesh axis runs over, the one named last changes fastest.
Arguments:
- view_data: bfloat16 [8, 4096, 2048], P('view', 'samp'), may hold values from -10 to 10
- init_coeffs: float32 [8, 2048, 128], P('view'), may hold values from -0.125 to 0.125
Outputs:
- shared_scores: float32 [4096, 128], P('samp')
- final_coeffs: float32 [8, 2048, 128], P('view', 'samp')
All inputs are finite; a program needn't handle non-finite values.
Results may differ from a plain program's by a relative error of at most 0.005.
Values may be sent and summed in bfloat16 or wider, within the bound.
No kernel may reach another device: no remote copies, remote signals or barrier semaphores. Data moves between devices by JAX's collectives and lax.ppermute only.
A program may use at most 128 MiB of HBM per device.

v0:
```python
import jax
import jax.numpy as jnp
from jax import lax
from jax.sharding import PartitionSpec as P

OUTER = 2
INNER = 2
NS_ITERS = 12
HIGH = lax.Precision.HIGHEST
ridge_weight = 0.1
step_size = 0.5


def newton_inverse(gram):
    size_k = gram.shape[0]
    eye_mat = jnp.eye(size_k, dtype=jnp.float32)
    shrunk = gram + jnp.trace(gram) / size_k * eye_mat
    scale = jnp.sqrt(jnp.sum(shrunk * shrunk))
    approx = shrunk / scale
    inverse = eye_mat
    for turn in range(NS_ITERS):
        factor = 0.5 * (3.0 * eye_mat - jnp.dot(inverse, approx, precision=HIGH))
        approx = jnp.dot(approx, factor, precision=HIGH)
        inverse = jnp.dot(factor, inverse, precision=HIGH)
    return (inverse, scale)


def make_scores(view_data, coeffs_low, total):
    local_sum = jnp.zeros((view_data.shape[1], coeffs_low.shape[2]), jnp.float32)
    for member in range(view_data.shape[0]):
        local_sum = local_sum + jnp.dot(
            view_data[member], coeffs_low[member], preferred_element_type=jnp.float32
        )
    summed = lax.psum(local_sum, "view")
    gram = lax.psum(jnp.dot(summed.T, summed, precision=HIGH), "samp")
    inverse, scale = newton_inverse(gram)
    return jnp.dot(summed, inverse, precision=HIGH) * jnp.sqrt(total / scale)


def grad_term(samples, weights_low, scores):
    resid = (jnp.dot(samples, weights_low, preferred_element_type=jnp.float32) - scores).astype(
        jnp.bfloat16
    )
    return lax.dot_general(
        samples, resid, (((0,), (0,)), ((), ())), preferred_element_type=jnp.float32
    )


def body(view_data, init_coeffs):
    total = view_data.shape[1] * lax.axis_size("samp")
    row_count = init_coeffs.shape[1] // lax.axis_size("samp")
    row_start = lax.axis_index("samp") * row_count
    own_coeffs = lax.dynamic_slice_in_dim(init_coeffs, row_start, row_count, 1)
    coeffs_low = init_coeffs.astype(jnp.bfloat16)
    scores = make_scores(view_data, coeffs_low, total)
    for outer_step in range(OUTER):
        for inner_step in range(INNER):
            terms = jnp.stack(
                [
                    grad_term(view_data[member], coeffs_low[member], scores)
                    for member in range(view_data.shape[0])
                ]
            )
            summed_grad = lax.psum_scatter(terms, "samp", scatter_dimension=1, tiled=True)
            own_coeffs = own_coeffs - step_size * (summed_grad / total + ridge_weight * own_coeffs)
            coeffs_low = lax.all_gather(own_coeffs.astype(jnp.bfloat16), "samp", axis=1, tiled=True)
        scores = make_scores(view_data, coeffs_low, total)
    return (scores, own_coeffs)


def solution(mesh):
    in_specs = (P("view", "samp", None), P("view", None, None))
    out_specs = (P("samp", None), P("view", "samp", None))
    return jax.shard_map(body, mesh=mesh, in_specs=in_specs, out_specs=out_specs, check_vma=False)
```

profile of v0, /device:TPU:0, one launch (start us, length us, event | category | flops | bytes accessed | tf_op | source)
XLA Modules:
  0.0 856.1 jit_solution(11644975215844309981)
XLA Ops:
  7.2 1.9 convert_element_type.42
  9.1 2.3 fusion.12
  12.9 35.1 %all-reduce.7.cloned.1.call-done = f32[512,128]{1,0:T(8,128)} async-done(((f32[512,128]{1,0:T(8,128)}), f32[512,128]{1,0:T(8,128)}) %all-reduce.7.cloned.1.call-update) | async-done | bytes 262160 | tf_op jit(solution)/shard_map/psum | solution.py:34
  48.0 2.2 fusion.165
  50.4 70.9 %all-reduce.9.cloned.1.call-done = f32[128,128]{1,0:T(8,128)} async-done(((f32[128,128]{1,0:T(8,128)}), f32[128,128]{1,0:T(8,128)}) %all-reduce.9.cloned.1.call-update) | async-done | bytes 65552 | tf_op jit(solution)/shard_map/psum | solution.py:35
  135.1 2.3 convolution_bitcast_fusion.6
  140.7 67.8 %reduce-scatter.5.cloned.1.call-done = f32[2,256,128]{1,2,0:T(8,128)} async-done(((f32[2,2048,128]{1,2,0:T(8,128)}), f32[2,256,128]{1,2,0:T(8,128)}) %reduce-scatter.5.cloned.1.call-update) | async-done | bytes 262160 | tf_op jit(solution)/shard_map/reduce_scatter | solution.py:64
  208.5 1.7 fusion.144
  210.3 39.2 %all-gather.5.cloned.1.call-done = bf16[2,2048,128]{1,2,0:T(8,128)(2,1)} async-done(((bf16[2,256,128]{1,2,0:T(8,128)(2,1)}), bf16[2,2048,128]{1,2,0:T(8,128)(2,1)}) %all-gather.5.cloned.1.call-update) | async-done | bytes 1048592 | tf_op jit(solution)/shard_map/all_gather | solution.py:66
  249.5 4.0 convolution_bitcast_fusion.4
  253.4 4.0 convolution_bitcast_fusion.5
  259.0 68.0 %reduce-scatter.7.cloned.1.call-done = f32[2,256,128]{1,2,0:T(8,128)} async-done(((f32[2,2048,128]{1,2,0:T(8,128)}), f32[2,256,128]{1,2,0:T(8,128)}) %reduce-scatter.7.cloned.1.call-update) | async-done | bytes 262160 | tf_op jit(solution)/shard_map/reduce_scatter | solution.py:64
  327.0 1.7 fusion.162
  328.7 39.1 %all-gather.7.cloned.1.call-done = bf16[2,2048,128]{1,2,0:T(8,128)(2,1)} async-done(((bf16[2,256,128]{1,2,0:T(8,128)(2,1)}), bf16[2,2048,128]{1,2,0:T(8,128)(2,1)}) %all-gather.7.cloned.1.call-update) | async-done | bytes 1048592 | tf_op jit(solution)/shard_map/all_gather | solution.py:66
  367.9 2.7 fusion.55
  370.6 3.1 fusion.164
  374.0 31.2 %all-reduce.11.cloned.1.call-done = f32[512,128]{0,1:T(8,128)} async-done(((f32[512,128]{0,1:T(8,128)}), f32[512,128]{0,1:T(8,128)}) %all-reduce.11.cloned.1.call-update) | async-done | bytes 262160 | tf_op jit(solution)/shard_map/psum | solution.py:34
  405.2 2.0 fusion.187
  407.3 71.1 %all-reduce.13.cloned.1.call-done = f32[128,128]{1,0:T(8,128)} async-done(((f32[128,128]{1,0:T(8,128)}), f32[128,128]{1,0:T(8,128)}) %all-reduce.13.cloned.1.call-update) | async-done | bytes 65552 | tf_op jit(solution)/shard_map/psum | solution.py:35
  492.3 2.3 convolution_bitcast_fusion.2
  496.7 69.1 %reduce-scatter.9.cloned.1.call-done = f32[2,256,128]{1,2,0:T(8,128)} async-done(((f32[2,2048,128]{1,2,0:T(8,128)}), f32[2,256,128]{1,2,0:T(8,128)}) %reduce-scatter.9.cloned.1.call-update) | async-done | bytes 262160 | tf_op jit(solution)/shard_map/reduce_scatter | solution.py:64
  567.5 39.2 %all-gather.9.cloned.1.call-done = bf16[2,2048,128]{1,2,0:T(8,128)(2,1)} async-done(((bf16[2,256,128]{1,2,0:T(8,128)(2,1)}), bf16[2,2048,128]{1,2,0:T(8,128)(2,1)}) %all-gather.9.cloned.1.call-update) | async-done | bytes 1048592 | tf_op jit(solution)/shard_map/all_gather | solution.py:66
  606.7 3.6 convolution_bitcast_fusion
  610.3 3.6 convolution_bitcast_fusion.1
  615.5 68.0 %reduce-scatter.11.cloned.1.call-done = f32[2,256,128]{1,2,0:T(8,128)} async-done(((f32[2,2048,128]{1,2,0:T(8,128)}), f32[2,256,128]{1,2,0:T(8,128)}) %reduce-scatter.11.cloned.1.call-update) | async-done | bytes 262160 | tf_op jit(solution)/shard_map/reduce_scatter | solution.py:64
  683.5 1.7 fusion.161
  685.3 39.1 %all-gather.11.cloned.1.call-done = bf16[2,2048,128]{1,2,0:T(8,128)(2,1)} async-done(((bf16[2,256,128]{1,2,0:T(8,128)(2,1)}), bf16[2,2048,128]{1,2,0:T(8,128)(2,1)}) %all-gather.11.cloned.1.call-update) | async-done | bytes 1048592 | tf_op jit(solution)/shard_map/all_gather | solution.py:66
  724.4 2.7 fusion
  727.1 3.1 fusion.46
  730.5 31.2 %all-reduce.15.cloned.1.call-done = f32[512,128]{0,1:T(8,128)} async-done(((f32[512,128]{0,1:T(8,128)}), f32[512,128]{0,1:T(8,128)}) %all-reduce.15.cloned.1.call-update) | async-done | bytes 262160 | tf_op jit(solution)/shard_map/psum | solution.py:34
  761.7 2.0 fusion.209
  764.6 70.2 %all-reduce.17.cloned.1.call-done = f32[128,128]{1,0:T(8,128)} async-done(((f32[128,128]{1,0:T(8,128)}), f32[128,128]{1,0:T(8,128)}) %all-reduce.17.cloned.1.call-update) | async-done | bytes 65552 | tf_op jit(solution)/shard_map/psum | solution.py:35
  (173 shorter events, 50.6 us)
Async XLA Ops:
  7.2 40.9 %all-reduce.7.cloned.1.call-start = ((), (), s32[]{:S(2)}) async-start(), calls=%async_computation.4 | async-start | bytes 524288 | tf_op jit(solution)/shard_map/psum | solution.py:34
  7.2 4.2 copy-start
  12.9 108.4 %all-reduce.9.cloned.1.call-start = ((), (), s32[]{:S(2)}) async-start(), calls=%async_computation.5 | async-start | bytes 131072 | tf_op jit(solution)/shard_map/psum | solution.py:35
  50.3 158.2 %reduce-scatter.5.cloned.1.call-start = ((), (), s32[]{:S(2)}) async-start(), calls=%async_computation.6 | async-start | bytes 2359296 | tf_op jit(solution)/shard_map/reduce_scatter | solution.py:64
  130.2 4.5 copy-start.4
  134.7 2.8 copy-start.1
  139.6 109.9 %all-gather.5.cloned.1.call-start = ((), (), s32[]{:S(2)}) async-start(), calls=%async_computation.7 | async-start | bytes 1179648 | tf_op jit(solution)/shard_map/all_gather | solution.py:66
  210.2 116.8 %reduce-scatter.7.cloned.1.call-start = ((), (), s32[]{:S(2)}) async-start(), calls=%async_computation.8 | async-start | bytes 2359296 | tf_op jit(solution)/shard_map/reduce_scatter | solution.py:64
  258.9 68.1 %copy-start.6 = (f32[2,256,128]{1,2,0:T(8,128)S(1)}, f32[2,256,128]{1,2,0:T(8,128)}, u32[]{:S(2)}) copy-start(f32[2,256,128]{1,2,0:T(8,128)} %reduce-scatter.5.cloned.1.call-done) | copy-start | bytes 786436
  258.9 109.0 %all-gather.7.cloned.1.call-start = ((), (), s32[]{:S(2)}) async-start(), calls=%async_computation.9 | async-start | bytes 1179648 | tf_op jit(solution)/shard_map/all_gather | solution.py:66
  328.7 76.5 %all-reduce.11.cloned.1.call-start = ((), (), s32[]{:S(2)}) async-start(), calls=%async_computation.10 | async-start | bytes 524288 | tf_op jit(solution)/shard_map/psum | solution.py:34
  367.9 2.7 copy-start.8
  373.7 104.7 %all-reduce.13.cloned.1.call-start = ((), (), s32[]{:S(2)}) async-start(), calls=%async_computation.11 | async-start | bytes 131072 | tf_op jit(solution)/shard_map/psum | solution.py:35
  407.3 158.5 %reduce-scatter.9.cloned.1.call-start = ((), (), s32[]{:S(2)}) async-start(), calls=%async_computation.12 | async-start | bytes 2359296 | tf_op jit(solution)/shard_map/reduce_scatter | solution.py:64
  487.4 4.5 copy-start.5
  491.9 2.8 copy-start.2
  496.7 110.0 %all-gather.9.cloned.1.call-start = ((), (), s32[]{:S(2)}) async-start(), calls=%async_computation.13 | async-start | bytes 1179648 | tf_op jit(solution)/shard_map/all_gather | solution.py:66
  567.5 116.0 %reduce-scatter.11.cloned.1.call-start = ((), (), s32[]{:S(2)}) async-start(), calls=%async_computation.14 | async-start | bytes 2359296 | tf_op jit(solution)/shard_map/reduce_scatter | solution.py:64
  615.4 68.1 %copy-start.7 = (f32[2,256,128]{1,2,0:T(8,128)S(1)}, f32[2,256,128]{1,2,0:T(8,128)}, u32[]{:S(2)}) copy-start(f32[2,256,128]{1,2,0:T(8,128)} %reduce-scatter.9.cloned.1.call-done) | copy-start | bytes 786436
  615.4 109.0 %all-gather.11.cloned.1.call-start = ((), (), s32[]{:S(2)}) async-start(), calls=%async_computation.15 | async-start | bytes 1179648 | tf_op jit(solution)/shard_map/all_gather | solution.py:66
  685.2 76.5 %all-reduce.15.cloned.1.call-start = ((), (), s32[]{:S(2)}) async-start(), calls=%async_computation.16 | async-start | bytes 524288 | tf_op jit(solution)/shard_map/psum | solution.py:34
  724.4 2.7 copy-start.9
  730.3 104.6 %all-reduce.17.cloned.1.call-start = ((), (), s32[]{:S(2)}) async-start(), calls=%async_computation.17 | async-start | bytes 131072 | tf_op jit(solution)/shard_map/psum | solution.py:35
  843.8 4.5 copy-start.3
Sparse Core Ops, SparseCore 0:
  13.0 35.0 all-reduce.6
  52.0 69.2 all-reduce.8
  139.7 68.8 reduce-scatter.4
  211.0 38.3 all-gather.4
  259.0 67.8 reduce-scatter.6
  329.4 38.4 all-gather.6
  373.9 31.2 all-reduce.10
  409.2 69.2 all-reduce.12
  496.8 68.9 reduce-scatter.8
  568.2 38.3 all-gather.8
  615.6 67.9 reduce-scatter.10
  686.0 38.3 all-gather.10
  730.4 31.2 all-reduce.14
  765.6 69.2 all-reduce.16
where the time goes:
time: 857 us; the launch traced here: 856 us
  waiting for transfers between devices  740 us (86%)
  matrix products  70.7 us (8%)
  other arithmetic  23.3 us (3%)
  between operations  19.3 us (2%)
    reduce_scatter x4, waiting for transfers between devices, body(): lax.psum_scatter(terms, 'samp', scatter_dimension=1, tiled=True)  273 us
    psum x3, waiting for transfers between devices, make_scores(): gram = lax.psum(jnp.dot(summed.T, summed, precision=HIGH), 'samp')  212 us
    all_gather x4, waiting for transfers between devices, body(): lax.all_gather(own_coeffs.astype(jnp.bfloat16), 'samp', axis=1, tiled=True)  157 us
    psum x3, waiting for transfers between devices, make_scores(): summed = lax.psum(local_sum, 'view')  97.5 us
    dot_general x8, matrix products, grad_term(): lax.dot_general(samples, resid, (((0,), (0,)), ((), ())), preferred_eleme...  20.6 us
  transfers between devices with their start and end apart: 14, of which 14 were waited for; matrix products, arithmetic and copies ran while one was open for 0% of the time, Pallas kernels for 0%

commit v1 on v0

--- a/solution.py
+++ b/solution.py
@@ -63,7 +63,15 @@
             )
             summed_grad = lax.psum_scatter(terms, "samp", scatter_dimension=1, tiled=True)
             own_coeffs = own_coeffs - step_size * (summed_grad / total + ridge_weight * own_coeffs)
-            coeffs_low = lax.all_gather(own_coeffs.astype(jnp.bfloat16), "samp", axis=1, tiled=True)
+            coeffs_low = jnp.concatenate(
+                lax.all_to_all(
+                    jnp.stack([own_coeffs.astype(jnp.bfloat16)] * lax.axis_size("samp")),
+                    "samp",
+                    0,
+                    0,
+                ),
+                axis=1,
+            )
         scores = make_scores(view_data, coeffs_low, total)
     return (scores, own_coeffs)
 

time: 857 us -> 802 us (0.936)
  waiting for transfers between devices: 740 us -> 582 us
  blocking collectives: 0 us -> 111 us
    all_gather x4 -> x0, waiting for transfers between devices: 157 us -> none  [body(): lax.all_gather(own_coeffs.astype(jnp.bfloat16), 'samp', axis=1, tiled=True)]
    all_to_all x0 -> x4, blocking collectives: none -> 111 us  [body(): lax.all_to_all(jnp.stack([own_coeffs.astype(jnp.bfloat16)] * lax.axis_siz...]
  transfers between devices with their start and end apart: 14 -> 10, of which waited for: 14 -> 10; matrix products, arithmetic and copies ran while one was open for 0% -> 0% of each run, Pallas kernels for 0% -> 0%
where the time goes in v1:
time: 802 us; the launch traced here: 801 us
  waiting for transfers between devices  582 us (73%)
  blocking collectives  111 us (14%)
  matrix products  63.1 us (8%)
  other arithmetic  20.7 us (3%)
  between operations  19.6 us (2%)
    reduce_scatter x4, waiting for transfers between devices, body(): lax.psum_scatter(terms, 'samp', scatter_dimension=1, tiled=True)  273 us
    psum x3, waiting for transfers between devices, make_scores(): gram = lax.psum(jnp.dot(summed.T, summed, precision=HIGH), 'samp')  212 us
    all_to_all x4, blocking collectives, body(): lax.all_to_all(jnp.stack([own_coeffs.astype(jnp.bfloat16)] * lax.axis_siz...  111 us
    psum x3, waiting for transfers between devices, make_scores(): summed = lax.psum(local_sum, 'view')  97.6 us
    dot_general x8, matrix products, grad_term(): lax.dot_general(samples, resid, (((0,), (0,)), ((), ())), preferred_eleme...  19.9 us
  transfers between devices with their start and end apart: 10, of which 10 were waited for; matrix products, arithmetic and copies ran while one was open for 0% of the time, Pallas kernels for 0%

profile of v1, /device:TPU:0, one launch (start us, length us, event | category | flops | bytes accessed | tf_op | source)
XLA Modules:
  0.0 801.4 jit_solution(9886404011825219546)
XLA Ops:
  7.2 1.9 convert_element_type.42
  9.1 2.3 fusion.12
  12.9 35.1 %all-reduce.7.cloned.1.call-done = f32[512,128]{1,0:T(8,128)} async-done(((f32[512,128]{1,0:T(8,128)}), f32[512,128]{1,0:T(8,128)}) %all-reduce.7.cloned.1.call-update) | async-done | bytes 262160 | tf_op jit(solution)/shard_map/psum | solution.py:34
  48.0 2.2 fusion.169
  50.4 70.9 %all-reduce.9.cloned.1.call-done = f32[128,128]{1,0:T(8,128)} async-done(((f32[128,128]{1,0:T(8,128)}), f32[128,128]{1,0:T(8,128)}) %all-reduce.9.cloned.1.call-update) | async-done | bytes 65552 | tf_op jit(solution)/shard_map/psum | solution.py:35
  123.4 1.5 multiply_reduce_fusion.2
  135.1 2.3 convolution_bitcast_fusion.6
  138.0 1.5 pad_maximum_fusion
  140.7 67.8 %reduce-scatter.5.cloned.1.call-done = f32[2,256,128]{1,2,0:T(8,128)} async-done(((f32[2,2048,128]{1,2,0:T(8,128)}), f32[2,256,128]{1,2,0:T(8,128)}) %reduce-scatter.5.cloned.1.call-update) | async-done | bytes 262160 | tf_op jit(solution)/shard_map/reduce_scatter | solution.py:64
  209.9 27.6 %all_to_all.20 = bf16[8,2,256,128]{3,2,1,0:T(8,128)(2,1)S(1)} all-to-all(bf16[8,2,256,128]{3,2,1,0:T(8,128)(2,1)S(1)} %stack.35), channel_id=1, replica_groups=mesh['view'=4,'samp'=8] {'samp'}, dimensions={0} | all-to-all | bytes 2097152 | tf_op jit(solution)/shard_map/all_to_all | solution.py:67
  237.5 3.8 convolution_bitcast_fusion.4
  241.4 3.8 convolution_bitcast_fusion.5
  245.2 1.5 pad_maximum_fusion.1
  246.7 67.9 %reduce-scatter.7.cloned.1.call-done = f32[2,256,128]{1,2,0:T(8,128)} async-done(((f32[2,2048,128]{1,2,0:T(8,128)}), f32[2,256,128]{1,2,0:T(8,128)}) %reduce-scatter.7.cloned.1.call-update) | async-done | bytes 262160 | tf_op jit(solution)/shard_map/reduce_scatter | solution.py:64
  316.1 27.9 %all_to_all.21 = bf16[8,2,256,128]{3,2,1,0:T(8,128)(2,1)S(1)} all-to-all(bf16[8,2,256,128]{3,2,1,0:T(8,128)(2,1)S(1)} %stack.39), channel_id=1, replica_groups=mesh['view'=4,'samp'=8] {'samp'}, dimensions={0} | all-to-all | bytes 2097152 | tf_op jit(solution)/shard_map/all_to_all | solution.py:67
  344.9 1.5 fusion.168
  346.5 31.4 %all-reduce.11.cloned.1.call-done = f32[512,128]{0,1:T(8,128)} async-done(((f32[512,128]{0,1:T(8,128)}), f32[512,128]{0,1:T(8,128)}) %all-reduce.11.cloned.1.call-update) | async-done | bytes 262160 | tf_op jit(solution)/shard_map/psum | solution.py:34
  377.8 2.0 fusion.191
  380.0 71.0 %all-reduce.13.cloned.1.call-done = f32[128,128]{1,0:T(8,128)} async-done(((f32[128,128]{1,0:T(8,128)}), f32[128,128]{1,0:T(8,128)}) %all-reduce.13.cloned.1.call-update) | async-done | bytes 65552 | tf_op jit(solution)/shard_map/psum | solution.py:35
  464.8 2.3 convolution_bitcast_fusion.2
  467.7 1.5 pad_maximum_fusion.2
  469.2 68.9 %reduce-scatter.9.cloned.1.call-done = f32[2,256,128]{1,2,0:T(8,128)} async-done(((f32[2,2048,128]{1,2,0:T(8,128)}), f32[2,256,128]{1,2,0:T(8,128)}) %reduce-scatter.9.cloned.1.call-update) | async-done | bytes 262160 | tf_op jit(solution)/shard_map/reduce_scatter | solution.py:64
  539.5 27.6 %all_to_all.22 = bf16[8,2,256,128]{3,2,1,0:T(8,128)(2,1)S(1)} all-to-all(bf16[8,2,256,128]{3,2,1,0:T(8,128)(2,1)S(1)} %stack.43), channel_id=1, replica_groups=mesh['view'=4,'samp'=8] {'samp'}, dimensions={0} | all-to-all | bytes 2097152 | tf_op jit(solution)/shard_map/all_to_all | solution.py:67
  567.2 3.4 convolution_bitcast_fusion
  570.6 3.4 convolution_bitcast_fusion.1
  574.1 1.5 pad_maximum_fusion.3
  575.6 67.9 %reduce-scatter.11.cloned.1.call-done = f32[2,256,128]{1,2,0:T(8,128)} async-done(((f32[2,2048,128]{1,2,0:T(8,128)}), f32[2,256,128]{1,2,0:T(8,128)}) %reduce-scatter.11.cloned.1.call-update) | async-done | bytes 262160 | tf_op jit(solution)/shard_map/reduce_scatter | solution.py:64
  645.0 27.9 %all_to_all.23 = bf16[8,2,256,128]{3,2,1,0:T(8,128)(2,1)S(1)} all-to-all(bf16[8,2,256,128]{3,2,1,0:T(8,128)(2,1)S(1)} %stack.47), channel_id=1, replica_groups=mesh['view'=4,'samp'=8] {'samp'}, dimensions={0} | all-to-all | bytes 2097152 | tf_op jit(solution)/shard_map/all_to_all | solution.py:67
  673.7 1.5 fusion.46
  675.6 31.1 %all-reduce.15.cloned.1.call-done = f32[512,128]{0,1:T(8,128)} async-done(((f32[512,128]{0,1:T(8,128)}), f32[512,128]{0,1:T(8,128)}) %all-reduce.15.cloned.1.call-update) | async-done | bytes 262160 | tf_op jit(solution)/shard_map/psum | solution.py:34
  706.7 2.0 fusion.213
  709.6 70.2 %all-reduce.17.cloned.1.call-done = f32[128,128]{1,0:T(8,128)} async-done(((f32[128,128]{1,0:T(8,128)}), f32[128,128]{1,0:T(8,128)}) %all-reduce.17.cloned.1.call-update) | async-done | bytes 65552 | tf_op jit(solution)/shard_map/psum | solution.py:35
  (177 shorter events, 48.5 us)
Async XLA Ops:
  7.2 40.9 %all-reduce.7.cloned.1.call-start = ((), (), s32[]{:S(2)}) async-start(), calls=%async_computation.8 | async-start | bytes 524288 | tf_op jit(solution)/shard_map/psum | solution.py:34
  7.2 4.2 copy-start
  12.9 108.4 %all-reduce.9.cloned.1.call-start = ((), (), s32[]{:S(2)}) async-start(), calls=%async_computation.9 | async-start | bytes 131072 | tf_op jit(solution)/shard_map/psum | solution.py:35
  50.3 158.2 %reduce-scatter.5.cloned.1.call-start = ((), (), s32[]{:S(2)}) async-start(), calls=%async_computation.10 | async-start | bytes 2359296 | tf_op jit(solution)/shard_map/reduce_scatter | solution.py:64
  130.2 4.5 copy-start.6
  134.7 2.8 copy-start.1
  139.6 175.1 %reduce-scatter.7.cloned.1.call-start = ((), (), s32[]{:S(2)}) async-start(), calls=%async_computation.11 | async-start | bytes 2359296 | tf_op jit(solution)/shard_map/reduce_scatter | solution.py:64
  246.7 68.0 %copy-start.8 = (f32[2,256,128]{1,2,0:T(8,128)S(1)}, f32[2,256,128]{1,2,0:T(8,128)}, u32[]{:S(2)}) copy-start(f32[2,256,128]{1,2,0:T(8,128)} %reduce-scatter.5.cloned.1.call-done) | copy-start | bytes 786436
  246.7 131.1 %all-reduce.11.cloned.1.call-start = ((), (), s32[]{:S(2)}) async-start(), calls=%async_computation.12 | async-start | bytes 524288 | tf_op jit(solution)/shard_map/psum | solution.py:34
  316.1 28.0 %copy-start.2 = (bf16[2,512,2048]{2,1,0:T(8,128)(2,1)S(1)}, bf16[2,512,2048]{2,1,0:T(8,128)(2,1)}, u32[]{:S(2)}) copy-start(bf16[2,512,2048]{2,1,0:T(8,128)(2,1)} %param.2) | copy-start | bytes 12582916
  346.4 104.5 %all-reduce.13.cloned.1.call-start = ((), (), s32[]{:S(2)}) async-start(), calls=%async_computation.13 | async-start | bytes 131072 | tf_op jit(solution)/shard_map/psum | solution.py:35
  379.9 158.2 %reduce-scatter.9.cloned.1.call-start = ((), (), s32[]{:S(2)}) async-start(), calls=%async_computation.14 | async-start | bytes 2359296 | tf_op jit(solution)/shard_map/reduce_scatter | solution.py:64
  459.9 4.5 copy-start.7
  464.4 2.8 copy-start.3
  469.2 174.4 %reduce-scatter.11.cloned.1.call-start = ((), (), s32[]{:S(2)}) async-start(), calls=%async_computation.15 | async-start | bytes 2359296 | tf_op jit(solution)/shard_map/reduce_scatter | solution.py:64
  575.5 68.0 %copy-start.9 = (f32[2,256,128]{1,2,0:T(8,128)S(1)}, f32[2,256,128]{1,2,0:T(8,128)}, u32[]{:S(2)}) copy-start(f32[2,256,128]{1,2,0:T(8,128)} %reduce-scatter.9.cloned.1.call-done) | copy-start | bytes 786436
  575.6 131.1 %all-reduce.15.cloned.1.call-start = ((), (), s32[]{:S(2)}) async-start(), calls=%async_computation.16 | async-start | bytes 524288 | tf_op jit(solution)/shard_map/psum | solution.py:34
  644.9 28.0 %copy-start.4 = (bf16[2,512,2048]{2,1,0:T(8,128)(2,1)S(1)}, bf16[2,512,2048]{2,1,0:T(8,128)(2,1)}, u32[]{:S(2)}) copy-start(bf16[2,512,2048]{2,1,0:T(8,128)(2,1)} %param.2) | copy-start | bytes 12582916
  675.3 104.5 %all-reduce.17.cloned.1.call-start = ((), (), s32[]{:S(2)}) async-start(), calls=%async_computation.17 | async-start | bytes 131072 | tf_op jit(solution)/shard_map/psum | solution.py:35
  788.7 4.5 copy-start.5
Sparse Core Ops, SparseCore 0:
  13.0 35.0 all-reduce.6
  52.0 69.2 all-reduce.8
  139.7 68.8 reduce-scatter.4
  246.8 67.8 reduce-scatter.6
  346.6 31.2 all-reduce.10
  381.7 69.2 all-reduce.12
  469.3 68.7 reduce-scatter.8
  575.7 67.8 reduce-scatter.10
  675.4 31.2 all-reduce.14
  710.5 69.2 all-reduce.16
